TPU v7x, 32 devices: a whole 2x2x4 slice. The times are simulated.
32 devices in a mesh: dp: 2 (over core), sx: 2 (over x), syz: 8 (over z, y).
Axes of the slice: x: 2, y: 2, z: 4, core: 2. Of those that a mesh axis runs over, the one named last changes fastest.
Arguments:
- volume: bfloat16 [2, 16, 32, 128, 256], P('dp', 'sx', 'syz'), may hold values from -80 to 80
- kernel: bfloat16 [3, 3, 3, 32, 256], replicated, may hold values from -1.36082763 to 1.36082763
Outputs:
- whitened: bfloat16 [2, 16, 32, 128, 256], P('dp', 'sx', 'syz')
All inputs are finite; a program needn't handle non-finite values.
Results may differ from a plain program's by a relative error of at most 0.006.
Values may be sent and summed in bfloat16 or wider, within the bound.
A program may use at most 128 MiB of HBM per device.

v0:
```python
import jax
import jax.numpy as jnp
from jax import lax
from jax.sharding import PartitionSpec as P

WGROUPS = 2
STEPS = 5


highest = lax.Precision.HIGHEST
epsilon = 1e-05


def padded(cells, sides, width):
    for axis, dim in sides:
        count = lax.axis_size(axis)
        ends = count - 1
        head = lax.slice_in_dim(cells, 0, width, axis=dim)
        tail = lax.slice_in_dim(cells, cells.shape[dim] - width, cells.shape[dim], axis=dim)
        cells = jnp.concatenate(
            [
                lax.ppermute(tail, axis, [(i, (i + 1) % count) for i in range(ends)]),
                cells,
                lax.ppermute(head, axis, [((i + 1) % count, i) for i in range(ends)]),
            ],
            axis=dim,
        )
    return cells


def whiten_matrix(covariance):
    identity = jnp.eye(covariance.shape[-1], dtype=jnp.float32)
    shifted = covariance + epsilon * identity
    frobenius = jnp.sqrt(jnp.sum(shifted * shifted, axis=(1, 2)))[:, None, None]
    iterate_y = shifted / frobenius
    iterate_z = jnp.broadcast_to(identity, shifted.shape)
    for number in range(STEPS):
        factor = 1.5 * identity - 0.5 * jnp.einsum(
            "gab,gbc->gac", iterate_z, iterate_y, precision=highest
        )
        iterate_y = jnp.einsum("gab,gbc->gac", iterate_y, factor, precision=highest)
        iterate_z = jnp.einsum("gab,gbc->gac", factor, iterate_z, precision=highest)
    return iterate_z / jnp.sqrt(frobenius)


def on_device(volume, kernel):
    extended = padded(volume, (("sx", 1), ("syz", 2)), 1)
    convolved = lax.conv_general_dilated(
        extended,
        kernel,
        (1, 1, 1),
        ((0, 0), (0, 0), (1, 1)),
        dimension_numbers=("NDHWC", "DHWIO", "NDHWC"),
        feature_group_count=volume.shape[4] // kernel.shape[3],
        preferred_element_type=jnp.float32,
    )
    hidden = convolved.astype(jnp.bfloat16)
    voxels = hidden.reshape(-1, WGROUPS, hidden.shape[4] // WGROUPS)
    local_count = float(voxels.shape[0])
    whole_count = local_count * lax.axis_size("dp") * lax.axis_size("sx") * lax.axis_size("syz")
    sum_first = jnp.sum(voxels, axis=0, dtype=jnp.float32)
    sum_second = jnp.einsum("nga,ngb->gab", voxels, voxels, preferred_element_type=jnp.float32)
    sum_first, sum_second = lax.psum((sum_first, sum_second), ("dp", "sx", "syz"))
    average = sum_first / whole_count
    covariance = sum_second / whole_count - average[:, :, None] * average[:, None, :]
    whitener = whiten_matrix(covariance)
    whitener_b = whitener.astype(jnp.bfloat16)
    shift = jnp.sum(whitener_b.astype(jnp.float32) * average[:, None, :], axis=2)
    result = (
        jnp.einsum("nga,gba->ngb", voxels, whitener_b, preferred_element_type=jnp.float32) - shift
    )
    return result.astype(jnp.bfloat16).reshape(volume.shape)


def solution(mesh):
    placed = (P("dp", "sx", "syz", None, None), P())
    return jax.shard_map(
        on_device,
        mesh=mesh,
        in_specs=placed,
        out_specs=P("dp", "sx", "syz", None, None),
        check_vma=False,
    )
```

profile of v0, /device:TPU:0, one launch (start us, length us, event | category | flops | bytes accessed | tf_op | source)
XLA Modules:
  0.0 594.6 jit_solution(5833961113538230310)
XLA Ops:
  6.5 0.0 all-reduce.2.cloned.1.call-start
  6.5 3.0 copy.10
  9.6 4.9 collective-permute-start
  14.5 1.3 collective-permute-start.1
  15.8 4.2 collective-permute-done
  20.0 4.1 collective-permute-done.1
  24.2 1.2 pad_maximum_fusion.3
  25.4 3.5 collective-permute-start.2
  28.9 1.3 collective-permute-start.3
  30.2 3.1 shard_map.30
  33.3 0.6 fusion.14
  33.9 0.7 fusion.13
  34.6 21.5 %collective-permute-done.2 = bf16[1,10,1,128,256]{3,4,2,1,0:T(8,128)(2,1)S(1)} collective-permute-done((bf16[1,10,1,128,256]{3,4,2,1,0:T(8,128)(2,1)}, bf16[1,10,1,128,256]{3,4,2,1,0:T(8,128)(2,1)S(1)}, u32[]{:S(2)}, u32[]{:S(2)}) %collective-permute-start.2) | collective-permute-done | bytes 655392 | tf_op jit(solution)/shard_map/ppermute | solution.py:22
  56.0 0.0 collective-permute-done.3
  56.0 3.1 pad_maximum_fusion
  59.2 58.0 %copy.13 = bf16[1,10,6,128,8,32]{5,0,4,3,2,1:T(2,128)(2,1)} copy(bf16[1,10,6,128,8,32]{3,5,4,2,1,0:T(8,128)(2,1)} %bitcast.38) | data formatting | bytes 7864320 | tf_op jit(solution)/shard_map/concatenate | solution.py:20
  117.2 0.0 copy-done
  117.2 312.3 %fusion.20 = (bf16[8,4,128,8,32]{4,3,2,1,0:T(8,128)(2,1)}, bf16[1,8,4,128,8,32]{5,0,4,3,2,1:T(2,128)(2,1)}) fusion(bf16[1,10,6,128,8,32]{5,0,4,3,2,1:T(2,128)(2,1)} %copy.13, bf16[3,3,3,32,8,32]{5,4,3,2,1,0:T(8,128)(2,1)S(1)} %copy-done), kind=kOutput, calls=%fused_computation.37 | convolution fusion | flops 1803550720 | bytes 8568832 | tf_op jit(solution)/shard_map/conv_general_dilated | solution.py:48
  429.4 11.3 %reshape.37 = bf16[4096,2,128]{2,1,0:T(2,128)(2,1)} reshape(bf16[8,4,128,8,32]{4,3,2,1,0:T(8,128)(2,1)} %get-tuple-element.11) | data formatting | bytes 4194304 | tf_op jit(solution)/shard_map/convert_element_type | solution.py:57
  440.7 4.7 copy.25
  445.4 1.4 fusion.21
  446.8 0.0 all-reduce.2.cloned.1.call-update
  446.8 0.0 copy-start.3
  446.8 0.0 copy-start.1
  446.8 0.0 copy-start.2
  446.8 36.1 %convert_reduce_fusion = f32[8,32]{1,0:T(8,128)S(1)} fusion(bf16[1,8,4,128,8,32]{5,0,4,3,2,1:T(2,128)(2,1)} %get-tuple-element.12), kind=kLoop, calls=%fused_computation.1 | loop fusion | flops 2096896 | bytes 2098176 | tf_op jit(solution)/shard_map/reduce_sum | solution.py:61
  482.9 0.1 reduce_sum.30
  483.0 41.4 %psum.15 = f32[2,128]{1,0:T(2,128)S(1)} all-reduce(f32[2,128]{1,0:T(2,128)S(1)} %reduce_sum.30), channel_id=1, replica_groups=mesh['dp'=2,'sx'=2,'syz'=8] {'dp','sx','syz'}, use_global_device_ids=true, to_apply=%region_2.0 | all-reduce | flops 256 | bytes 2048 | tf_op jit(solution)/shard_map/psum | solution.py:63
  524.4 48.3 %all-reduce.2.cloned.1.call-done = f32[2,128,128]{2,1,0:T(8,128)} async-done(((f32[2,128,128]{2,1,0:T(8,128)}), f32[2,128,128]{2,1,0:T(8,128)}) %all-reduce.2.cloned.1.call-update) | async-done | bytes 131088 | tf_op jit(solution)/shard_map/psum | solution.py:63
  572.7 1.1 multiply_reduce_fusion.1
  573.8 0.0 copy-done.2
  573.8 1.3 fusion.7
  575.1 0.3 fusion.10
  575.4 1.2 fusion.16
  576.6 0.3 fusion.6
  576.9 0.3 fusion.23
  577.2 0.3 fusion.22
  577.4 0.3 fusion.5
  577.7 0.3 fusion.25
  578.0 0.3 fusion.24
  578.3 0.3 fusion.4
  578.5 0.3 fusion.27
  578.8 0.3 fusion.26
  579.1 0.3 fusion.3
  579.4 0.4 multiply_reduce_fusion
  579.7 2.0 fusion.1
  581.7 3.2 reshape.36
  585.0 2.7 copy.20
  (6 shorter events, 0.1 us)
Async XLA Ops:
  6.5 566.2 %all-reduce.2.cloned.1.call-start = ((), (), s32[]{:S(2)}) async-start(), calls=%async_computation | async-start | bytes 262144 | tf_op jit(solution)/shard_map/psum | solution.py:63
  9.6 10.4 %collective-permute-start = (bf16[1,1,4,128,256]{3,4,2,1,0:T(8,128)(2,1)S(1)}, bf16[1,1,4,128,256]{3,4,2,1,0:T(8,128)(2,1)S(1)}, u32[]{:S(2)}, u32[]{:S(2)}) collective-permute-start(bf16[1,1,4,128,256]{3,4,2,1,0:T(8,128)(2,1)S(1)} %get-tuple-element.7), channel_id=1, source_target_pairs={{0,8},{1,9},{2,10},{3,11},{4,12},{5,13},{6,14},{7,15},{16,24},{17,... | collective-permute-start | bytes 786440 | tf_op jit(solution)/shard_map/ppermute | solution.py:22
  14.5 9.7 %collective-permute-start.1 = (bf16[1,1,4,128,256]{3,4,2,1,0:T(8,128)(2,1)S(1)}, bf16[1,1,4,128,256]{3,4,2,1,0:T(8,128)(2,1)S(1)}, u32[]{:S(2)}, u32[]{:S(2)}) collective-permute-start(bf16[1,1,4,128,256]{3,4,2,1,0:T(8,128)(2,1)S(1)} %get-tuple-element.8), channel_id=1, source_target_pairs={{8,0},{9,1},{10,2},{11,3},{12,4},{13,5},{14,6},{15,7},{24,16},{25,... | collective-permute-start | bytes 786440 | tf_op jit(solution)/shard_map/ppermute | solution.py:24
  25.4 30.6 %collective-permute-start.2 = (bf16[1,10,1,128,256]{3,4,2,1,0:T(8,128)(2,1)}, bf16[1,10,1,128,256]{3,4,2,1,0:T(8,128)(2,1)S(1)}, u32[]{:S(2)}, u32[]{:S(2)}) collective-permute-start(bf16[1,10,1,128,256]{3,4,2,1,0:T(8,128)(2,1)} %get-tuple-element.5), channel_id=1, source_target_pairs={{0,1},{1,2},{2,3},{3,4},{4,5},{5,6},{6,7},{8,9},{9,10},{10,11},{11... | collective-permute-start | bytes 1966088 | tf_op jit(solution)/shard_map/ppermute | solution.py:22
  28.9 27.2 %collective-permute-start.3 = (bf16[1,10,1,128,256]{3,4,2,1,0:T(8,128)(2,1)}, bf16[1,10,1,128,256]{3,4,2,1,0:T(8,128)(2,1)}, u32[]{:S(2)}, u32[]{:S(2)}) collective-permute-start(bf16[1,10,1,128,256]{3,4,2,1,0:T(8,128)(2,1)} %get-tuple-element.6), channel_id=1, source_target_pairs={{1,0},{2,1},{3,2},{4,3},{5,4},{6,5},{7,6},{9,8},{10,9},{11,10},{12... | collective-permute-start | bytes 1966088 | tf_op jit(solution)/shard_map/ppermute | solution.py:24
  59.2 58.0 %copy-start = (bf16[3,3,3,32,8,32]{5,4,3,2,1,0:T(8,128)(2,1)S(1)}, bf16[3,3,3,32,8,32]{5,4,3,2,1,0:T(8,128)(2,1)}, u32[]{:S(2)}) copy-start(bf16[3,3,3,32,8,32]{5,4,3,2,1,0:T(8,128)(2,1)} %shard_map.30) | copy-start | bytes 1327108
  446.8 125.9 %copy-start.3 = (f32[128,128]{1,0:T(8,128)S(1)}, f32[128,128]{1,0:T(8,128)}, u32[]{:S(2)}) copy-start(f32[128,128]{1,0:T(8,128)} %get-tuple-element.15) | copy-start | bytes 196612
  446.8 127.0 %copy-start.1 = (f32[128,128]{1,0:T(8,128)S(1)}, f32[128,128]{1,0:T(8,128)}, u32[]{:S(2)}) copy-start(f32[128,128]{1,0:T(8,128)} %get-tuple-element.16) | copy-start | bytes 196612
  446.8 127.0 %copy-start.2 = (f32[128,128]{1,0:T(8,128)S(1)}, f32[128,128]{1,0:T(8,128)}, u32[]{:S(2)}) copy-start(f32[128,128]{1,0:T(8,128)} %fusion.14) | copy-start | bytes 196612
Sparse Core Ops, SparseCore 0:
  446.9 125.6 all-reduce.1
where the time goes:
time: 601 us; the launch traced here: 595 us
  matrix products  321 us (53%)
  local copies, waits for them, and re-layouts  86.2 us (14%)
  waiting for transfers between devices  78.1 us (13%)
  other arithmetic  42.9 us (7%)
  blocking collectives  41.4 us (7%)
  between operations  13.6 us (2%)
  starting transfers between devices  10.9 us (2%)
    conv_general_dilated x1, matrix products, on_device(): lax.conv_general_dilated(extended, kernel, (1, 1, 1), ((0, 0), (0, 0), (1...  312 us
    concatenate x1, local copies, waits for them, and re-layouts, padded(): jnp.concatenate([lax.ppermute(tail, axis, [(i, (i + 1) % count) for i in...  58 us
    psum x1, waiting for transfers between devices, on_device(): lax.psum((sum_first, sum_second), ('dp', 'sx', 'syz'))  48.3 us
    psum x1, blocking collectives, on_device(): lax.psum((sum_first, sum_second), ('dp', 'sx', 'syz'))  41.4 us
    reduce_sum x1, other arithmetic, on_device(): sum_first = jnp.sum(voxels, axis=0, dtype=jnp.float32)  36.1 us
    ppermute x2, waiting for transfers between devices, padded(): lax.ppermute(tail, axis, [(i, (i + 1) % count) for i in range(ends)])  25.7 us
    convert_element_type x2, local copies, waits for them, and re-layouts, on_device(): hidden = convolved.astype(jnp.bfloat16)  16 us
  transfers between devices with their start and end apart: 5, of which 4 were waited for; matrix products, arithmetic and copies ran while one was open for 7% of the time, Pallas kernels for 0%

commit v1 on v0

v1 whole, which is shorter than its diff:
```python
import functools

import jax
import jax.numpy as jnp
from jax import lax
from jax.experimental import pallas as pl
from jax.experimental.pallas import tpu as pltpu
from jax.sharding import PartitionSpec as P

WGROUPS = 2
STEPS = 5
epsilon = 1e-05
highest = lax.Precision.HIGHEST
MESH = pl.DeviceIdType.MESH
F32 = jnp.float32
BF16 = jnp.bfloat16
OTHERS = ((-1, 0), (1, 0), (-1, -1), (-1, 1), (1, -1), (1, 1))


def fma(a, b):
    return jnp.dot(a, b, preferred_element_type=F32)


def fdot(a, b):
    return jnp.dot(a, b, precision=highest, preferred_element_type=F32)


def main_kernel(
    sizes, stages, parts, whole_count,
    v_ref, k_ref, hid_out, white_ref, shift_ref,
    xs, wd, acc, hid, gram, red, got, give, got_pair, fin, got_fin,
    load_sem, store_sem, send_y, recv_y, send_o, recv_o,
    pair_send, pair_recv, tree_send, tree_recv,
):
    nx, ny = sizes
    X, Y, Z, C = v_ref.shape[1:]
    GC = k_ref.shape[1]
    WG = C // WGROUPS
    me_d = lax.axis_index("dp")
    me_x = lax.axis_index("sx")
    me_y = lax.axis_index("syz")

    def flip(axis, bit):
        me = lax.axis_index(axis)
        return {axis: me + bit - 2 * bit * ((me // bit) % 2)}

    def there(dx, dy):
        ok = None
        for d, me, n in ((dx, me_x, nx), (dy, me_y, ny)):
            if d:
                t = (me >= 1) if d < 0 else (me < n - 1)
                ok = t if ok is None else ok & t
        return ok

    def target(dx, dy):
        return (me_d, me_x + dx, me_y + dy)

    load = pltpu.make_async_copy(
        v_ref.at[0], xs.at[pl.ds(1, X), pl.ds(1, Y), :, pl.ds(C, C)], load_sem)
    load.start()

    barrier = pltpu.get_barrier_semaphore()
    near = ((0, -1), (0, 1)) + OTHERS
    for dx, dy in near:
        @pl.when(there(dx, dy))
        def _(dx=dx, dy=dy):
            pl.semaphore_signal(barrier, inc=1, device_id=target(dx, dy), device_id_type=MESH)
    far = [flip("dp", 1)] + [flip(a, b) for a, b in stages]
    for who in far:
        pl.semaphore_signal(barrier, inc=1, device_id=who, device_id_type=MESH)
    has_x = [jnp.where(there(d, 0), 1, 0) for d in (-1, 1)]
    has_y = [jnp.where(there(0, d), 1, 0) for d in (-1, 1)]
    around = (1 + has_x[0] + has_x[1]) * (1 + has_y[0] + has_y[1]) - 1
    pl.semaphore_wait(barrier, around + len(far))

    def span(d, n):
        if d == 0:
            return pl.ds(0, n), pl.ds(1, n)
        if d < 0:
            return pl.ds(0, 1), pl.ds(n + 1, 1)
        return pl.ds(n - 1, 1), pl.ds(0, 1)

    def halo(dx, dy, send, recv):
        sx, tx = span(dx, X)
        sy, ty = span(dy, Y)
        return pltpu.make_async_remote_copy(
            src_ref=v_ref.at[0, sx, sy],
            dst_ref=xs.at[tx, ty, :, pl.ds(C, C)],
            send_sem=send, recv_sem=recv,
            device_id=target(dx, dy), device_id_type=MESH)

    halos = [(0, -1, send_y.at[0], recv_y.at[0]), (0, 1, send_y.at[1], recv_y.at[1])]
    halos += [(dx, dy, send_o.at[i], recv_o.at[i]) for i, (dx, dy) in enumerate(OTHERS)]
    for dx, dy, s, r in halos:
        @pl.when(there(dx, dy))
        def _(dx=dx, dy=dy, s=s, r=r):
            halo(dx, dy, s, r).start()

        @pl.when(jnp.logical_not(there(-dx, -dy)))
        def _(dx=dx, dy=dy):
            tx, ty = span(dx, X)[1], span(dy, Y)[1]
            xs[tx, ty, :, pl.ds(C, C)] = jnp.zeros((tx.size, ty.size, Z, C), BF16)

    lanes = lax.broadcasted_iota(jnp.int32, (GC, C), 1) // GC

    @pl.loop(0, k_ref.shape[0])
    def _(t):
        w = k_ref[t].astype(F32)
        for g in range(C // GC):
            wd[t, pl.ds(g * GC, GC), :] = jnp.where(lanes == g, w, 0.0).astype(BF16)

    rows = lax.broadcasted_iota(jnp.int32, (Z, C), 0)

    def shifted(px, py):
        v = xs[px, py, :, pl.ds(C, C)].astype(F32)
        xs[px, py, :, pl.ds(0, C)] = jnp.where(rows == 0, 0.0, pltpu.roll(v, 1, 0)).astype(BF16)
        xs[px, py, :, pl.ds(2 * C, C)] = jnp.where(
            rows == Z - 1, 0.0, pltpu.roll(v, Z - 1, 0)).astype(BF16)

    load.wait()

    @pl.loop(1, X + 1)
    def _(px):
        for py in range(1, Y + 1):
            shifted(px, py)

    def weight(a, b):
        return wd[pl.ds(((a + 1) * 3 + b + 1) * 3, 3)].reshape(3 * C, C)

    def inner(px, y0, n):
        return xs[px, pl.ds(y0, n)].reshape(n * Z, 3 * C)

    def plane(x, offsets):
        full = sum(fma(inner(x + 1 + a, 1, Y), weight(a, 0)) for a in offsets)
        acc[x] = full
        if Y > 1:
            m = (Y - 1) * Z
            acc[x, pl.ds(Z, m)] += sum(fma(inner(x + 1 + a, 1, Y - 1), weight(a, -1)) for a in offsets)
            acc[x, pl.ds(0, m)] += sum(fma(inner(x + 1 + a, 2, Y - 1), weight(a, 1)) for a in offsets)

    if X == 1:
        plane(0, (0,))
    else:
        plane(0, (0, 1))
        if X > 2:
            @pl.loop(1, X - 1)
            def _(x):
                plane(x, (-1, 0, 1))
        plane(X - 1, (-1, 0))

    for dx, dy, s, r in halos:
        @pl.when(there(-dx, -dy))
        def _(dx=dx, dy=dy, s=s, r=r):
            halo(dx, dy, s, r).wait_recv()

    @pl.loop(0, X + 2)
    def _(px):
        for py in (0, Y + 1):
            shifted(px, py)

    @pl.loop(1, Y + 1)
    def _(py):
        for px in (0, X + 1):
            shifted(px, py)

    for px, x, a in ((0, 0, -1), (X + 1, X - 1, 1)):
        acc[x] += sum(fma(inner(px, b + 1, Y), weight(a, b)) for b in (-1, 0, 1))
    for py, y, b in ((0, 0, -1), (Y + 1, Y - 1, 1)):
        for a in (-1, 0, 1):
            x0, n = (0, X) if a == 0 else ((1, X - 1) if a < 0 else (0, X - 1))
            if n:
                lhs = xs[pl.ds(x0 + 1 + a, n), py].reshape(n * Z, 3 * C)
                acc[pl.ds(x0, n), pl.ds(y * Z, Z)] += fma(lhs, weight(a, b)).reshape(n, Z, C)

    gram[...] = jnp.zeros_like(gram)

    @pl.loop(0, X)
    def _(x):
        h = acc[x].astype(BF16)
        hid[x] = h
        gram[pl.ds(0, C)] += lax.dot_general(
            h, h, (((0,), (0,)), ((), ())), preferred_element_type=F32)
        gram[pl.ds(C, 8)] += jnp.sum(h.astype(F32).reshape(Y * Z // 8, 8, C), axis=0)

    store = pltpu.make_async_copy(hid, hid_out, store_sem)
    store.start()

    mine = me_d == 0
    low = gram[pl.ds(0, WG), pl.ds(0, WG)]
    high = gram[pl.ds(WG, WG), pl.ds(WG, WG)]
    low_sum = gram[pl.ds(C, 8), pl.ds(0, WG)]
    high_sum = gram[pl.ds(C, 8), pl.ds(WG, WG)]
    give[pl.ds(0, WG)] = jnp.where(mine, high, low)
    give[pl.ds(WG, 8)] = jnp.where(mine, high_sum, low_sum)
    pair = flip("dp", 1)
    swap = pltpu.make_async_remote_copy(
        src_ref=give, dst_ref=got_pair, send_sem=pair_send.at[0], recv_sem=pair_recv.at[0],
        device_id=pair, device_id_type=MESH)
    swap.start()
    own = jnp.where(mine, low, high)
    own_sum = jnp.where(mine, low_sum, high_sum)
    swap.wait()
    red[0, pl.ds(0, WG)] = own + got_pair[pl.ds(0, WG)]
    red[0, pl.ds(WG, 8)] = own_sum + got_pair[pl.ds(WG, 8)]

    count = len(stages)

    def leg(step, stream):
        axis, bit = stages[(step + stream) % count]
        part = pl.ds(*parts[stream])
        return pltpu.make_async_remote_copy(
            src_ref=red.at[step, part], dst_ref=got.at[step, part],
            send_sem=tree_send.at[step, stream], recv_sem=tree_recv.at[step, stream],
            device_id=flip(axis, bit), device_id_type=MESH)

    for step in range(count):
        for stream in range(len(parts)):
            leg(step, stream).start()
        for stream in range(len(parts)):
            leg(step, stream).wait_recv()
            part = pl.ds(*parts[stream])
            red[step + 1, part] = red[step, part] + got[step, part]

    average = jnp.sum(red[count, pl.ds(WG, 8)], axis=0, keepdims=True) / whole_count
    across = jnp.broadcast_to(average, (WG, WG))
    down = across.T
    covariance = red[count, pl.ds(0, WG)] / whole_count - down * across
    identity = jnp.where(
        lax.broadcasted_iota(jnp.int32, (WG, WG), 0) == lax.broadcasted_iota(jnp.int32, (WG, WG), 1),
        1.0, 0.0).astype(F32)
    moved = covariance + epsilon * identity
    square = jnp.sum(jnp.sum(moved * moved, axis=1, keepdims=True), axis=0, keepdims=True)
    frobenius = jnp.sqrt(square)
    y = moved / frobenius
    z = None
    for number in range(STEPS):
        p = 1.5 * identity - 0.5 * (y if z is None else fdot(z, y))
        if number < STEPS - 1:
            y = fdot(y, p)
        z = p if z is None else fdot(p, z)
    whitener = z / jnp.sqrt(frobenius)
    turned = whitener.T.astype(BF16).astype(F32)
    fin[pl.ds(0, WG)] = turned
    fin[pl.ds(WG, 8)] = jnp.broadcast_to(jnp.sum(turned * down, axis=0, keepdims=True), (8, WG))
    swap = pltpu.make_async_remote_copy(
        src_ref=fin, dst_ref=got_fin, send_sem=pair_send.at[1], recv_sem=pair_recv.at[1],
        device_id=pair, device_id_type=MESH)
    swap.start()
    own = fin[...]
    swap.wait()
    other = got_fin[...]
    first = jnp.where(mine, own, other)
    second = jnp.where(mine, other, own)
    white_ref[...] = jnp.zeros_like(white_ref)
    white_ref[pl.ds(0, WG), pl.ds(0, WG)] = first[:WG].astype(BF16)
    white_ref[pl.ds(WG, WG), pl.ds(WG, WG)] = second[:WG].astype(BF16)
    shift_ref[:, pl.ds(0, WG)] = first[WG:]
    shift_ref[:, pl.ds(WG, WG)] = second[WG:]

    store.wait()
    for step in range(count):
        for stream in range(len(parts)):
            leg(step, stream).wait_send()
    for dx, dy, s, r in halos:
        @pl.when(there(dx, dy))
        def _(dx=dx, dy=dy, s=s, r=r):
            halo(dx, dy, s, r).wait_send()


def apply_kernel(h_ref, w_ref, s_ref, o_ref):
    X, M, C = h_ref.shape
    result = fma(h_ref[...].reshape(X * M, C), w_ref[...]) - s_ref[0:1, :]
    o_ref[...] = result.astype(BF16).reshape(o_ref.shape)


def on_device(sizes, volume, kernel):
    nd, nx, ny = sizes
    X, Y, Z, C = volume.shape[1:]
    GC = kernel.shape[3]
    WG = C // WGROUPS
    stages = []
    for axis, n in (("sx", nx), ("syz", ny)):
        bit = 1
        while bit < n:
            stages.append((axis, bit))
            bit *= 2
    streams = min(4, len(stages))
    blocks = (WG + 8) // 8
    edges = [8 * (blocks * i // streams) for i in range(streams + 1)]
    parts = [(edges[i], edges[i + 1] - edges[i]) for i in range(streams)]
    whole_count = float(X * Y * Z * nd * nx * ny)
    R = WG + 8
    count = len(stages)
    dma = pltpu.SemaphoreType.DMA
    hidden, white, shift = pl.pallas_call(
        functools.partial(main_kernel, (nx, ny), tuple(stages), tuple(parts), whole_count),
        out_shape=(
            jax.ShapeDtypeStruct((X, Y * Z, C), BF16),
            jax.ShapeDtypeStruct((C, C), BF16),
            jax.ShapeDtypeStruct((8, C), F32),
        ),
        in_specs=[pl.BlockSpec(memory_space=pl.ANY), pl.BlockSpec(memory_space=pltpu.VMEM)],
        out_specs=(
            pl.BlockSpec(memory_space=pl.ANY),
            pl.BlockSpec(memory_space=pltpu.VMEM),
            pl.BlockSpec(memory_space=pltpu.VMEM),
        ),
        scratch_shapes=[
            pltpu.VMEM((X + 2, Y + 2, Z, 3 * C), BF16),
            pltpu.VMEM((27, C, C), BF16),
            pltpu.VMEM((X, Y * Z, C), F32),
            pltpu.VMEM((X, Y * Z, C), BF16),
            pltpu.VMEM((C + 8, C), F32),
            pltpu.VMEM((count + 1, R, WG), F32),
            pltpu.VMEM((count, R, WG), F32),
            pltpu.VMEM((R, WG), F32),
            pltpu.VMEM((R, WG), F32),
            pltpu.VMEM((R, WG), F32),
            pltpu.VMEM((R, WG), F32),
            dma, dma, dma((2,)), dma((2,)), dma((len(OTHERS),)), dma((len(OTHERS),)),
            dma((2,)), dma((2,)), dma((count, streams)), dma((count, streams)),
        ],
        compiler_params=pltpu.CompilerParams(
            collective_id=0, has_side_effects=True, vmem_limit_bytes=56 * 2**20),
        name="conv_moments",
    )(volume, kernel.reshape(27, GC, C))
    result = pl.pallas_call(
        apply_kernel,
        grid=(X // 2,),
        out_shape=jax.ShapeDtypeStruct((X, Y, Z, C), BF16),
        in_specs=[
            pl.BlockSpec((2, Y * Z, C), lambda i: (i, 0, 0)),
            pl.BlockSpec((C, C), lambda i: (0, 0)),
            pl.BlockSpec((8, C), lambda i: (0, 0)),
        ],
        out_specs=pl.BlockSpec((2, Y, Z, C), lambda i: (i, 0, 0, 0)),
        name="apply",
    )(hidden, white, shift)
    return result.reshape(volume.shape)


def solution(mesh):
    sizes = (mesh.shape["dp"], mesh.shape["sx"], mesh.shape["syz"])
    placed = (P("dp", "sx", "syz", None, None), P())
    return jax.shard_map(
        functools.partial(on_device, sizes),
        mesh=mesh,
        in_specs=placed,
        out_specs=P("dp", "sx", "syz", None, None),
        check_vma=False,
    )
```

time: 601 us -> 63.8 us (0.11); the launches traced: 595 us -> 63.5 us
  matrix products: 321 us -> 0 us
  local copies, waits for them, and re-layouts: 86.2 us -> 0 us
  waiting for transfers between devices: 78.1 us -> 0 us
  Pallas kernels: 0 us -> 63.5 us
  other arithmetic: 42.9 us -> 0 us
  blocking collectives: 41.4 us -> 0 us
  between operations: 13.6 us -> 0.01 us
  starting transfers between devices: 10.9 us -> 0 us
    conv_general_dilated x1 -> x0, matrix products: 312 us -> none  [on_device(): lax.conv_general_dilated(extended, kernel, (1, 1, 1), ((0, 0), (0, 0), (1...]
    pallas_call x0 -> x2, Pallas kernels: none -> 63.5 us  [the longest x1 59.2 us: on_device(): pl.pallas_call(functools.partial(main_kernel, (nx, ny), tuple(stages), tu...]
    concatenate x1 -> x0, local copies, waits for them, and re-layouts: 58 us -> none  [padded(): jnp.concatenate([lax.ppermute(tail, axis, [(i, (i + 1) % count) for i in...]
    psum x1 -> x0, waiting for transfers between devices: 48.3 us -> none  [on_device(): lax.psum((sum_first, sum_second), ('dp', 'sx', 'syz'))]
    psum x1 -> x0, blocking collectives: 41.4 us -> none  [on_device(): lax.psum((sum_first, sum_second), ('dp', 'sx', 'syz'))]
    reduce_sum x2 -> x0, other arithmetic: 37.2 us -> none  [the longest x1 36.1 us: on_device(): sum_first = jnp.sum(voxels, axis=0, dtype=jnp.float32)]
    ppermute x4 -> x0, waiting for transfers between devices: 29.8 us -> none  [the longest x2 25.7 us: padded(): lax.ppermute(tail, axis, [(i, (i + 1) % count) for i in range(ends)])]
    convert_element_type x2 -> x0, local copies, waits for them, and re-layouts: 16 us -> none  [on_device(): hidden = convolved.astype(jnp.bfloat16)]
  transfers between devices with their start and end apart: 5 -> 0, of which waited for: 4 -> 0; matrix products, arithmetic and copies ran while one was open for 7% -> 0% of each run, Pallas kernels for 0% -> 0%
where the time goes in v1:
time: 63.8 us; the launch traced here: 63.5 us
  Pallas kernels  63.5 us (100%)
    pallas_call x1, Pallas kernels, on_device(): pl.pallas_call(functools.partial(main_kernel, (nx, ny), tuple(stages), tu...  59.2 us
    pallas_call x1, Pallas kernels, on_device(): pl.pallas_call(apply_kernel, grid=(X // 2,), out_shape=jax.ShapeDtypeStru...  4.35 us

profile of v1, /device:TPU:0, one launch (start us, length us, event | category | flops | bytes accessed | tf_op | source)
XLA Modules:
  0.0 63.5 jit_solution(6334159505683678475)
XLA Ops:
  0.0 59.2 %conv_moments.1 = (bf16[8,512,256]{2,1,0:T(8,128)(2,1)}, bf16[256,256]{1,0:T(8,128)(2,1)}, f32[8,256]{1,0:T(8,128)}) custom-call(bf16[1,8,4,128,256]{4,3,2,1,0:T(8,128)(2,1)} %v_ref.1, bf16[27,32,256]{2,1,0:T(8,128)(2,1)} %bitcast.2), custom_call_target="tpu_custom_call" | custom-call | tf_op jit(solution)/shard_map/conv_moments/pallas_call | solution.py:295
  59.2 4.3 %apply.1 = bf16[8,4,128,256]{3,2,1,0:T(8,128)(2,1)} custom-call(bf16[8,512,256]{2,1,0:T(8,128)(2,1)} %get-tuple-element.8.h_ref, bf16[256,256]{1,0:T(8,128)(2,1)} %get-tuple-element.9.w_ref, f32[8,256]{1,0:T(8,128)} %get-tuple-element.10.s_ref), custom_call_target="tpu_custom_call" | custom-call | tf_op jit(solution)/shard_map/apply/pallas_call | solution.py:327

commit v2 on v1

--- a/solution.py
+++ b/solution.py
@@ -14,7 +14,7 @@
 MESH = pl.DeviceIdType.MESH
 F32 = jnp.float32
 BF16 = jnp.bfloat16
-OTHERS = ((-1, 0), (1, 0), (-1, -1), (-1, 1), (1, -1), (1, 1))
+SIDES = (-1, 1)
 
 
 def fma(a, b):
@@ -29,7 +29,8 @@
     sizes, stages, parts, whole_count,
     v_ref, k_ref, hid_out, white_ref, shift_ref,
     xs, wd, acc, hid, gram, red, got, give, got_pair, fin, got_fin,
-    load_sem, store_sem, send_y, recv_y, send_o, recv_o,
+    halo_y, halo_x, halo_c,
+    load_sem, store_sem, send_y, recv_y, send_x, recv_x, send_c, recv_c,
     pair_send, pair_recv, tree_send, tree_recv,
 ):
     nx, ny = sizes
@@ -60,7 +61,7 @@
     load.start()
 
     barrier = pltpu.get_barrier_semaphore()
-    near = ((0, -1), (0, 1)) + OTHERS
+    near = ((0, -1), (0, 1), (-1, 0), (1, 0))
     for dx, dy in near:
         @pl.when(there(dx, dy))
         def _(dx=dx, dy=dy):
@@ -70,36 +71,60 @@
         pl.semaphore_signal(barrier, inc=1, device_id=who, device_id_type=MESH)
     has_x = [jnp.where(there(d, 0), 1, 0) for d in (-1, 1)]
     has_y = [jnp.where(there(0, d), 1, 0) for d in (-1, 1)]
-    around = (1 + has_x[0] + has_x[1]) * (1 + has_y[0] + has_y[1]) - 1
+    around = has_x[0] + has_x[1] + has_y[0] + has_y[1]
     pl.semaphore_wait(barrier, around + len(far))
 
-    def span(d, n):
-        if d == 0:
-            return pl.ds(0, n), pl.ds(1, n)
-        if d < 0:
-            return pl.ds(0, 1), pl.ds(n + 1, 1)
-        return pl.ds(n - 1, 1), pl.ds(0, 1)
-
-    def halo(dx, dy, send, recv):
-        sx, tx = span(dx, X)
-        sy, ty = span(dy, Y)
+    def remote(src, dst, send, recv, dx, dy):
         return pltpu.make_async_remote_copy(
-            src_ref=v_ref.at[0, sx, sy],
-            dst_ref=xs.at[tx, ty, :, pl.ds(C, C)],
-            send_sem=send, recv_sem=recv,
+            src_ref=src, dst_ref=dst, send_sem=send, recv_sem=recv,
             device_id=target(dx, dy), device_id_type=MESH)
 
-    halos = [(0, -1, send_y.at[0], recv_y.at[0]), (0, 1, send_y.at[1], recv_y.at[1])]
-    halos += [(dx, dy, send_o.at[i], recv_o.at[i]) for i, (dx, dy) in enumerate(OTHERS)]
-    for dx, dy, s, r in halos:
-        @pl.when(there(dx, dy))
-        def _(dx=dx, dy=dy, s=s, r=r):
-            halo(dx, dy, s, r).start()
-
-        @pl.when(jnp.logical_not(there(-dx, -dy)))
-        def _(dx=dx, dy=dy):
-            tx, ty = span(dx, X)[1], span(dy, Y)[1]
-            xs[tx, ty, :, pl.ds(C, C)] = jnp.zeros((tx.size, ty.size, Z, C), BF16)
+    def piece(x, side):
+        d = SIDES[1 - side]
+        return remote(v_ref.at[0, x, Y - 1 if d > 0 else 0], halo_y.at[side, x],
+                      send_y.at[side, x], recv_y.at[side, x], 0, d)
+
+    def face(side):
+        d = SIDES[1 - side]
+        return remote(v_ref.at[0, X - 1 if d > 0 else 0], halo_x.at[side],
+                      send_x.at[side], recv_x.at[side], d, 0)
+
+    def corner(side, side_y):
+        d = SIDES[1 - side]
+        return remote(halo_y.at[side_y, X - 1 if d > 0 else 0], halo_c.at[side, side_y],
+                      send_c.at[side, side_y], recv_c.at[side, side_y], d, 0)
+
+    early = [0] if X == 1 else [0, X - 1]
+    order = early + list(range(1, X - 1))
+
+    for x in early:
+        for side in (0, 1):
+            @pl.when(there(0, SIDES[1 - side]))
+            def _(x=x, side=side):
+                piece(x, side).start()
+    for side in (0, 1):
+        @pl.when(there(SIDES[1 - side], 0))
+        def _(side=side):
+            face(side).start()
+    for x in order[len(early):]:
+        for side in (0, 1):
+            @pl.when(there(0, SIDES[1 - side]))
+            def _(x=x, side=side):
+                piece(x, side).start()
+
+    for side in (0, 1):
+        @pl.when(jnp.logical_not(there(0, SIDES[side])))
+        def _(side=side):
+            halo_y[side] = jnp.zeros((X, Z, C), BF16)
+
+        @pl.when(jnp.logical_not(there(SIDES[side], 0)))
+        def _(side=side):
+            halo_x[side] = jnp.zeros((Y, Z, C), BF16)
+
+        for side_y in (0, 1):
+            @pl.when(jnp.logical_not(there(SIDES[side], SIDES[side_y])))
+            def _(side=side, side_y=side_y):
+                halo_c[side, side_y] = jnp.zeros((Z, C), BF16)
 
     lanes = lax.broadcasted_iota(jnp.int32, (GC, C), 1) // GC
 
@@ -111,8 +136,11 @@
 
     rows = lax.broadcasted_iota(jnp.int32, (Z, C), 0)
 
-    def shifted(px, py):
-        v = xs[px, py, :, pl.ds(C, C)].astype(F32)
+    def shifted(px, py, source=None):
+        v = xs[px, py, :, pl.ds(C, C)] if source is None else source
+        if source is not None:
+            xs[px, py, :, pl.ds(C, C)] = v
+        v = v.astype(F32)
         xs[px, py, :, pl.ds(0, C)] = jnp.where(rows == 0, 0.0, pltpu.roll(v, 1, 0)).astype(BF16)
         xs[px, py, :, pl.ds(2 * C, C)] = jnp.where(
             rows == Z - 1, 0.0, pltpu.roll(v, Z - 1, 0)).astype(BF16)
@@ -130,57 +158,87 @@
     def inner(px, y0, n):
         return xs[px, pl.ds(y0, n)].reshape(n * Z, 3 * C)
 
-    def plane(x, offsets):
+    def taps(x, offsets):
         full = sum(fma(inner(x + 1 + a, 1, Y), weight(a, 0)) for a in offsets)
-        acc[x] = full
+        if Y == 1:
+            return full, None, None
+        after = sum(fma(inner(x + 1 + a, 1, Y - 1), weight(a, -1)) for a in offsets)
+        before = sum(fma(inner(x + 1 + a, 2, Y - 1), weight(a, 1)) for a in offsets)
+        return full, after, before
+
+    def plane(x, offsets, more=False):
+        full, after, before = taps(x, offsets)
+        if more:
+            acc[x] += full
+        else:
+            acc[x] = full
         if Y > 1:
             m = (Y - 1) * Z
-            acc[x, pl.ds(Z, m)] += sum(fma(inner(x + 1 + a, 1, Y - 1), weight(a, -1)) for a in offsets)
-            acc[x, pl.ds(0, m)] += sum(fma(inner(x + 1 + a, 2, Y - 1), weight(a, 1)) for a in offsets)
-
-    if X == 1:
-        plane(0, (0,))
-    else:
-        plane(0, (0, 1))
-        if X > 2:
-            @pl.loop(1, X - 1)
-            def _(x):
-                plane(x, (-1, 0, 1))
+            acc[x, pl.ds(Z, m)] += after
+            acc[x, pl.ds(0, m)] += before
+
+    plane(0, (0, 1) if X > 1 else (0,))
+
+    for x in early:
+        for side_y in (0, 1):
+            @pl.when(there(0, SIDES[side_y]))
+            def _(x=x, side_y=side_y):
+                piece(x, side_y).wait_recv()
+    for side in (0, 1):
+        for side_y in (0, 1):
+            @pl.when(there(SIDES[1 - side], 0) & there(0, SIDES[side_y]))
+            def _(side=side, side_y=side_y):
+                corner(side, side_y).start()
+
+    if X > 2:
+        @pl.loop(1, X - 1)
+        def _(x):
+            plane(x, (-1, 0, 1))
+    if X > 1:
         plane(X - 1, (-1, 0))
 
-    for dx, dy, s, r in halos:
-        @pl.when(there(-dx, -dy))
-        def _(dx=dx, dy=dy, s=s, r=r):
-            halo(dx, dy, s, r).wait_recv()
-
-    @pl.loop(0, X + 2)
-    def _(px):
-        for py in (0, Y + 1):
-            shifted(px, py)
-
-    @pl.loop(1, Y + 1)
-    def _(py):
-        for px in (0, X + 1):
-            shifted(px, py)
-
-    for px, x, a in ((0, 0, -1), (X + 1, X - 1, 1)):
-        acc[x] += sum(fma(inner(px, b + 1, Y), weight(a, b)) for b in (-1, 0, 1))
-    for py, y, b in ((0, 0, -1), (Y + 1, Y - 1, 1)):
-        for a in (-1, 0, 1):
-            x0, n = (0, X) if a == 0 else ((1, X - 1) if a < 0 else (0, X - 1))
-            if n:
-                lhs = xs[pl.ds(x0 + 1 + a, n), py].reshape(n * Z, 3 * C)
-                acc[pl.ds(x0, n), pl.ds(y * Z, Z)] += fma(lhs, weight(a, b)).reshape(n, Z, C)
+    for side in (0, 1):
+        @pl.when(there(SIDES[side], 0))
+        def _(side=side):
+            face(side).wait_recv()
+        for side_y in (0, 1):
+            @pl.when(there(SIDES[side], SIDES[side_y]))
+            def _(side=side, side_y=side_y):
+                corner(side, side_y).wait_recv()
+        px = (X + 1) * side
+
+        @pl.loop(0, Y)
+        def _(y, side=side, px=px):
+            shifted(px, y + 1, halo_x[side, y])
+        for side_y in (0, 1):
+            shifted(px, (Y + 1) * side_y, halo_c[side, side_y])
+    plane(0, (-1,), True)
+    plane(X - 1, (1,), True)
 
     gram[...] = jnp.zeros_like(gram)
-
-    @pl.loop(0, X)
-    def _(x):
-        h = acc[x].astype(BF16)
-        hid[x] = h
+    for x in early:
+        for side_y in (0, 1):
+            shifted(x + 1, (Y + 1) * side_y, halo_y[side_y, x])
+    pair_x = 2 if X % 2 == 0 else 1
+    for x in range(0, X, pair_x):
+        for new in range(x if x else 1, x + pair_x + 1):
+            if (x == 0 or new > x) and new < X - 1:
+                for side_y in (0, 1):
+                    @pl.when(there(0, SIDES[side_y]))
+                    def _(new=new, side_y=side_y):
+                        piece(new, side_y).wait_recv()
+                    shifted(new + 1, (Y + 1) * side_y, halo_y[side_y, new])
+        for py, y, b in ((0, 0, -1), (Y + 1, Y - 1, 1)):
+            add = sum(
+                fma(xs[pl.ds(x + 1 + a, pair_x), py].reshape(pair_x * Z, 3 * C), weight(a, b))
+                for a in (-1, 0, 1))
+            acc[pl.ds(x, pair_x), pl.ds(y * Z, Z)] += add.reshape(pair_x, Z, C)
+        h = acc[pl.ds(x, pair_x)].astype(BF16)
+        hid[pl.ds(x, pair_x)] = h
+        h = h.reshape(pair_x * Y * Z, C)
         gram[pl.ds(0, C)] += lax.dot_general(
             h, h, (((0,), (0,)), ((), ())), preferred_element_type=F32)
-        gram[pl.ds(C, 8)] += jnp.sum(h.astype(F32).reshape(Y * Z // 8, 8, C), axis=0)
+        gram[pl.ds(C, 8)] += jnp.sum(h.astype(F32).reshape(pair_x * Y * Z // 8, 8, C), axis=0)
 
     store = pltpu.make_async_copy(hid, hid_out, store_sem)
     store.start()
@@ -261,10 +319,19 @@
     for step in range(count):
         for stream in range(len(parts)):
             leg(step, stream).wait_send()
-    for dx, dy, s, r in halos:
-        @pl.when(there(dx, dy))
-        def _(dx=dx, dy=dy, s=s, r=r):
-            halo(dx, dy, s, r).wait_send()
+    for side in (0, 1):
+        @pl.when(there(0, SIDES[1 - side]))
+        def _(side=side):
+            for x in range(X):
+                piece(x, side).wait_send()
+
+        @pl.when(there(SIDES[1 - side], 0))
+        def _(side=side):
+            face(side).wait_send()
+        for side_y in (0, 1):
+            @pl.when(there(SIDES[1 - side], 0) & there(0, SIDES[side_y]))
+            def _(side=side, side_y=side_y):
+                corner(side, side_y).wait_send()
 
 
 def apply_kernel(h_ref, w_ref, s_ref, o_ref):
@@ -317,7 +384,10 @@
             pltpu.VMEM((R, WG), F32),
             pltpu.VMEM((R, WG), F32),
             pltpu.VMEM((R, WG), F32),
-            dma, dma, dma((2,)), dma((2,)), dma((len(OTHERS),)), dma((len(OTHERS),)),
+            pltpu.VMEM((2, X, Z, C), BF16),
+            pltpu.VMEM((2, Y, Z, C), BF16),
+            pltpu.VMEM((2, 2, Z, C), BF16),
+            dma, dma, dma((2, X)), dma((2, X)), dma((2,)), dma((2,)), dma((2, 2)), dma((2, 2)),
             dma((2,)), dma((2,)), dma((count, streams)), dma((count, streams)),
         ],
         compiler_params=pltpu.CompilerParams(

time: 63.8 us -> 65.6 us (1.028)
  Pallas kernels: 63.5 us -> 65.4 us
    pallas_call x1, Pallas kernels: 59.2 us -> 61 us  [on_device(): pl.pallas_call(functools.partial(main_kernel, (nx, ny), tuple(stages), tu...]
where the time goes in v2:
time: 65.6 us; the launch traced here: 65.4 us
  Pallas kernels  65.4 us (100%)
    pallas_call x1, Pallas kernels, on_device(): pl.pallas_call(functools.partial(main_kernel, (nx, ny), tuple(stages), tu...  61 us
    pallas_call x1, Pallas kernels, on_device(): pl.pallas_call(apply_kernel, grid=(X // 2,), out_shape=jax.ShapeDtypeStru...  4.35 us

profile of v2, /device:TPU:0, one launch (start us, length us, event | category | flops | bytes accessed | tf_op | source)
XLA Modules:
  0.0 65.4 jit_solution(14745058124910553729)
XLA Ops:
  0.0 61.0 %conv_moments.1 = (bf16[8,512,256]{2,1,0:T(8,128)(2,1)}, bf16[256,256]{1,0:T(8,128)(2,1)}, f32[8,256]{1,0:T(8,128)}) custom-call(bf16[1,8,4,128,256]{4,3,2,1,0:T(8,128)(2,1)} %v_ref.1, bf16[27,32,256]{2,1,0:T(8,128)(2,1)} %bitcast.2), custom_call_target="tpu_custom_call" | custom-call | tf_op jit(solution)/shard_map/conv_moments/pallas_call | solution.py:362
  61.0 4.4 %apply.1 = bf16[8,4,128,256]{3,2,1,0:T(8,128)(2,1)} custom-call(bf16[8,512,256]{2,1,0:T(8,128)(2,1)} %get-tuple-element.8.h_ref, bf16[256,256]{1,0:T(8,128)(2,1)} %get-tuple-element.9.w_ref, f32[8,256]{1,0:T(8,128)} %get-tuple-element.10.s_ref), custom_call_target="tpu_custom_call" | custom-call | tf_op jit(solution)/shard_map/apply/pallas_call | solution.py:397
